TPU v7x, 128 devices: a whole 4x4x4 slice. The times are simulated.
128 devices in a mesh: gx: 4 (over y), gy: 32 (over z, x, core).
Axes of the slice: x: 4, y: 4, z: 4, core: 2. Of those that a mesh axis runs over, the one named last changes fastest.
Arguments:
- patches: bfloat16 [256, 4096, 256], P(('gx', 'gy')), may hold values from -6 to 6
- start_frames: float32 [256, 256, 256], P(('gx', 'gy')), may hold values from -6 to 6
- pair_ends: int32 [1024, 2], P('gx'), may hold values from 0 to 255, as said below
- margin_blocks: int32 [1024, 2, 4], P('gx'), may hold values from 0 to 31, as said below
Outputs:
- aligned: bfloat16 [256, 4096, 256], P(('gx', 'gy'))
- final_frames: float32 [256, 256, 256], P(('gx', 'gy'))
- frame_total: float32 [256, 256], replicated
Inputs may be any that keep to these rules, and one draw needn't show every extreme that they name: `pair_ends`: both ends of a pair lie in the owner's group of 64 patches (patches of the devices with the owner's gx index), on distinct patches; at most 1 ends of one owner's pairs lie on any one device, and ends on one device are of distinct patches; some device holds exactly 1 of some owner's ends. Every patch is an end of some pair. Patch p lives on device p // 2, devices counted with gx slowest. Patch degrees are uneven. `margin_blocks`: the 4 blocks of one end are distinct.
All inputs are finite; a program needn't handle non-finite values.
Results may differ from a plain program's by a relative error of at most 0.012.
The roundings to bfloat16 on the way count: a program that leaves them out, or rounds other values in their place, can miss the bound.
Values may be sent and summed in bfloat16 or wider, within the bound.
No kernel may reach another device: no remote copies, remote signals or barrier semaphores. Data moves between devices by JAX's collectives and lax.ppermute only.
A program may use at most 128 MiB of HBM per device.

v0:
```python
import jax
import jax.numpy as jnp
from jax import lax
from jax.sharding import Mesh
from jax.sharding import PartitionSpec as P

BLOCK = 128
SWEEPS = 2
NS_STEPS = 5
GY = ("gy_0", "gy_1", "gy_2")
GX_GY = ("gx", "gy_0", "gy_1", "gy_2")
coef_first = 3.4445
coef_second = -4.775
coef_third = 2.0315


def rows_for(lines, size):
    spare = -len(lines) % size
    return jnp.pad(lines, [(0, spare)] + [(0, 0)] * (lines.ndim - 1))


def from_everyone(value, axis):
    size = lax.axis_size(axis)
    return lax.all_to_all(
        jnp.broadcast_to(value[None], (size, *value.shape)), axis, 0, 0, tiled=True
    )


def in_order(parts, dim):
    parts = jnp.moveaxis(parts, 0, dim)
    dims = parts.shape
    return parts.reshape(*dims[:dim], dims[dim] * dims[dim + 1], *dims[dim + 2 :])


def whole_of(value, axes, dim):
    far, near = axes
    parts = from_everyone(from_everyone(value, far), near)
    return in_order(parts.swapaxes(0, 1).reshape(-1, *value.shape), dim)


def in_blocks(value, dim, size):
    dims = value.shape
    parts = value.reshape(*dims[:dim], size, dims[dim] // size, *dims[dim + 1 :])
    return jnp.moveaxis(parts, dim, 0)


def sent_and_summed(value, axis, dim):
    parts = in_blocks(value, dim, lax.axis_size(axis))
    arrived = lax.all_to_all(parts, axis, split_axis=0, concat_axis=0, tiled=True)
    return arrived.sum(axis=0)


def sum_by_axis(value, axes, dim):
    far, near = axes
    parts = in_blocks(value, dim, lax.axis_size(far))
    nearer = sent_and_summed(parts, near, dim + 1)
    arrived = lax.all_to_all(nearer, far, split_axis=0, concat_axis=0, tiled=True)
    return arrived.sum(axis=0)


def sum_by_parts(value, axes):
    lines = value.reshape(-1, value.shape[-1])
    padded = rows_for(lines, lax.axis_size(axes[0]) * lax.axis_size(axes[1]))
    whole = whole_of(sum_by_axis(padded, axes, 0), axes, 0)
    return lax.slice_in_dim(whole, 0, len(lines)).reshape(value.shape)


def newton_schulz(matrix):
    scaling = lax.rsqrt(jnp.sum(matrix * matrix, axis=(-2, -1), keepdims=True) + 1e-06)
    matrix = matrix * scaling
    for repeat_index in range(NS_STEPS):
        square = jnp.einsum("...ij,...kj->...ik", matrix, matrix, precision=lax.Precision.HIGHEST)
        polynom = coef_second * square + coef_third * jnp.einsum(
            "...ij,...jk->...ik", square, square, precision=lax.Precision.HIGHEST
        )
        matrix = coef_first * matrix + jnp.einsum(
            "...ij,...jk->...ik", polynom, matrix, precision=lax.Precision.HIGHEST
        )
    return matrix


def local(patches, start_frames, pair_ends, margin_blocks):
    group_size = lax.axis_size(GY)
    my_column = lax.axis_index(GY)
    my_group = lax.axis_index("gx")
    per_device, row_count, width = patches.shape
    pairs_owned = pair_ends.shape[0] // group_size
    ends_count = 2 * pairs_owned
    capacity = -(-ends_count // group_size)
    group_base = my_group * (group_size * per_device)
    local_ids = pair_ends.reshape(group_size, ends_count) - group_base
    partner_ids = pair_ends[:, ::-1].reshape(group_size, ends_count) - group_base
    device_of = local_ids // per_device
    patch_of = local_ids % per_device
    positions = jnp.arange(ends_count, dtype=jnp.int32)
    earlier = positions[None, :] < positions[:, None]
    same_device = device_of[:, :, None] == device_of[:, None, :]
    order_rank = jnp.sum(same_device & earlier[None], axis=2)
    slot_numbers = jnp.arange(capacity, dtype=jnp.int32)
    mine = device_of == my_column
    selected = (mine[:, None, :] & (order_rank[:, None, :] == slot_numbers[None, :, None])).astype(
        jnp.int32
    )
    slot_live = jnp.sum(selected, axis=2)
    slot_patch = jnp.sum(selected * patch_of[:, None, :], axis=2)
    slot_partner = jnp.sum(selected * partner_ids[:, None, :], axis=2)
    blocks_group = margin_blocks.reshape(group_size, ends_count, -1)
    slot_blocks = jnp.sum(selected[:, :, :, None] * blocks_group[:, None, :, :], axis=2)
    offsets = jnp.arange(BLOCK, dtype=jnp.int32)
    row_index = (
        slot_patch[:, :, None, None] * row_count
        + slot_blocks[:, :, :, None] * BLOCK
        + offsets[None, None, None, :]
    ).reshape(-1)
    packed = jnp.take(patches.reshape(per_device * row_count, width), row_index, axis=0)
    packed = packed.reshape(group_size, capacity, -1, width)
    received = lax.all_to_all(packed, GY, split_axis=0, concat_axis=0, tiled=True)
    my_devices = jnp.take(device_of, my_column, axis=0)
    my_ranks = jnp.take(order_rank, my_column, axis=0)
    my_rows = received[my_devices, my_ranks].reshape(pairs_owned, 2, -1, width)
    gram = jnp.einsum(
        "pri,prj->pij", my_rows[:, 1], my_rows[:, 0], preferred_element_type=jnp.float32
    )
    rotation = newton_schulz(gram)
    q_ends = jnp.stack([jnp.swapaxes(rotation, 1, 2), rotation], axis=1).reshape(
        ends_count, width, width
    )
    device_numbers = jnp.arange(group_size, dtype=jnp.int32)
    placing = (
        (my_devices[None, None, :] == device_numbers[:, None, None])
        & (my_ranks[None, None, :] == slot_numbers[None, :, None])
    ).astype(jnp.float32)
    patch_numbers = jnp.arange(per_device, dtype=jnp.int32)
    slot_weights = (
        ((slot_patch[None] == patch_numbers[:, None, None]) & (slot_live[None] > 0))
        .astype(jnp.float32)
        .reshape(per_device, -1)
    )
    frames = newton_schulz(start_frames)
    rotation_slots = jnp.einsum("dce,eij->dcij", placing, q_ends, precision=lax.Precision.HIGHEST)
    rotation_recv = lax.all_to_all(
        rotation_slots, GY, split_axis=0, concat_axis=0, tiled=True
    ).reshape(-1, width, width)
    partner_flat = slot_partner.reshape(-1)
    for iteration in range(SWEEPS):
        frames_low = frames.astype(jnp.bfloat16)
        everyone = lax.all_gather(frames_low, GY, axis=0, tiled=True)
        partner = jnp.take(everyone, partner_flat, axis=0).astype(jnp.float32)
        estimate = jnp.einsum(
            "sij,sjk->sik", rotation_recv, partner, precision=lax.Precision.HIGHEST
        )
        summed = jnp.einsum("ps,sik->pik", slot_weights, estimate, precision=lax.Precision.HIGHEST)
        frames = newton_schulz(frames + summed)
    total_frame = sum_by_parts(jnp.sum(frames, axis=0), (("gx", "gy_0", "gy_1"), "gy_2"))
    gauge = newton_schulz(total_frame)
    final_frames = jnp.einsum("pij,kj->pik", frames, gauge, precision=lax.Precision.HIGHEST)
    aligned = jnp.einsum(
        "prd,pdk->prk",
        patches,
        final_frames.astype(jnp.bfloat16),
        preferred_element_type=jnp.float32,
    )
    return (aligned.astype(jnp.bfloat16), final_frames, total_frame)


def solution(mesh):
    torus = Mesh(mesh.devices.reshape(mesh.shape["gx"], 4, 4, 2), ("gx", "gy_0", "gy_1", "gy_2"))
    return jax.shard_map(
        local,
        mesh=torus,
        in_specs=(P(GX_GY, None, None), P(GX_GY, None, None), P("gx", None), P("gx", None, None)),
        out_specs=(P(GX_GY, None, None), P(GX_GY, None, None), P()),
        check_vma=False,
    )
```

profile of v0, /device:TPU:1, one launch (start us, length us, event | category | flops | bytes accessed | tf_op | source)
XLA Modules:
  0.0 567.2 jit_solution(18084156238551683727)
XLA Ops:
  9.0 0.9 copy.197
  11.0 63.5 %gather_fusion = bf16[16384,256]{1,0:T(8,128)(2,1)} fusion(bf16[8192,256]{1,0:T(8,128)(2,1)} %bitcast.206, s32[16384]{0:T(1024)S(1)} %broadcast_clamp_fusion), kind=kCustom, calls=%fused_computation.2 | custom fusion | bytes 16842752 | tf_op jit(solution)/shard_map/jit(_take)/gather | solution.py:115
  74.7 8.1 %broadcast_select_fusion = bf16[32,1,512,256]{3,2,1,0:T(8,128)(2,1)} fusion(bf16[32,1,512,256]{3,2,1,0:T(8,128)(2,1)} %bitcast.207, pred[32,512]{1,0:T(8,128)(4,1)S(1)} %compare_and_fusion), kind=kLoop, calls=%fused_computation.12 | loop fusion | flops 4194304 | bytes 16793600 | tf_op jit(solution)/shard_map/jit(_take)/select_n | solution.py:115
  82.8 9.6 %all-to-all-start = ((bf16[32,1,512,256]{3,2,1,0:T(8,128)(2,1)}), bf16[32,1,512,256]{3,2,1,0:T(8,128)(2,1)}, u32[]{:S(2)}, u32[]{:S(2)}) async-start(bf16[32,1,512,256]{3,2,1,0:T(8,128)(2,1)} %broadcast_select_fusion), calls=%async_computation | async-start | bytes 16777216 | tf_op jit(solution)/shard_map/all_to_all | solution.py:117
  102.6 1.4 fusion.142
  104.4 94.2 %all-to-all-done = bf16[32,1,512,256]{3,2,1,0:T(8,128)(2,1)} async-done(((bf16[32,1,512,256]{3,2,1,0:T(8,128)(2,1)}), bf16[32,1,512,256]{3,2,1,0:T(8,128)(2,1)}, u32[]{:S(2)}, u32[]{:S(2)}) %all-to-all-start) | async-done | bytes 8388640 | tf_op jit(solution)/shard_map/all_to_all | solution.py:117
  198.6 6.6 %gather_fusion.1 = bf16[16,512,256]{2,1,0:T(8,128)(2,1)} fusion(bf16[32,1,512,256]{3,2,1,0:T(8,128)(2,1)} %all-to-all-done, s32[16]{0:T(128)S(1)} %fusion.125), kind=kCustom, calls=%fused_computation.3 | custom fusion | bytes 8388736 | tf_op jit(solution)/shard_map/gather | solution.py:120
  205.2 3.2 multiply_reduce_fusion
  208.4 2.8 fusion.48
  211.2 2.1 fusion.149
  213.4 2.6 multiply_add_fusion.4
  216.0 2.1 fusion.150
  218.1 2.1 fusion.151
  220.3 2.6 multiply_add_fusion.3
  222.9 2.1 fusion.152
  225.0 2.1 fusion.153
  227.1 2.4 multiply_add_fusion.2
  229.6 2.1 fusion.154
  231.7 2.5 fusion.155
  234.2 2.4 multiply_add_fusion.1
  236.7 2.1 fusion.156
  238.8 2.1 fusion.157
  240.9 2.4 multiply_add_fusion
  243.4 2.7 copy.201
  246.1 2.0 pad_maximum_fusion
  248.5 5.7 %fusion.15 = f32[32,1,256,256]{3,0,2,1:T(8,128)S(1)} fusion(f32[16,256,256]{2,1,0:T(8,128)S(1)} %bitcast.209, s32[16]{0:T(128)S(1)} %select_reduce_fusion.1, pred[16]{0:T(512)(128)(4,1)S(1)} %broadcast_compare_fusion.1), kind=kOutput, calls=%fused_computation.22 | convolution fusion | flops 402654208 | bytes 12582992 | tf_op jit(solution)/shard_map/dce,eij->dcij/dot_general | solution.py:140
  254.2 8.1 %copy.204 = f32[32,1,256,256]{3,2,1,0:T(8,128)} copy(f32[32,1,256,256]{3,0,2,1:T(8,128)S(1)} %fusion.15) | data formatting | bytes 16777216 | tf_op jit(solution)/shard_map/dce,eij->dcij/dot_general | solution.py:140
  262.3 20.2 %all-to-all-start.1 = ((f32[32,1,256,256]{3,2,1,0:T(8,128)}), f32[32,1,256,256]{3,2,1,0:T(8,128)}, u32[]{:S(2)}, u32[]{:S(2)}) async-start(f32[32,1,256,256]{3,2,1,0:T(8,128)} %copy.204), calls=%async_computation.1 | async-start | bytes 16777216 | tf_op jit(solution)/shard_map/all_to_all | solution.py:141
  282.6 6.2 %gather_fusion.2 = bf16[32,256,256]{2,1,0:T(8,128)(2,1)} fusion(bf16[64,256,256]{2,1,0:T(8,128)(2,1)} %all-gather.3.cloned.1.call-done, s32[1024]{0:T(1024)S(1)} %pad_clamp_fusion), kind=kCustom, calls=%fused_computation.clone | custom fusion | bytes 8388736 | tf_op jit(solution)/shard_map/jit(_take)/gather | solution.py:148
  288.8 94.4 %all-to-all-done.1 = f32[32,1,256,256]{3,2,1,0:T(8,128)} async-done(((f32[32,1,256,256]{3,2,1,0:T(8,128)}), f32[32,1,256,256]{3,2,1,0:T(8,128)}, u32[]{:S(2)}, u32[]{:S(2)}) %all-to-all-start.1) | async-done | bytes 8388640 | tf_op jit(solution)/shard_map/all_to_all | solution.py:141
  383.2 8.8 %fusion.2 = f32[32,256,256]{2,1,0:T(8,128)S(1)} fusion(f32[32,1,256,256]{3,2,1,0:T(8,128)} %all-to-all-done.1, bf16[32,256,256]{2,1,0:T(8,128)(2,1)} %gather_fusion.2, pred[32]{0:T(512)(128)(4,1)S(1)} %compare_and_fusion.1), kind=kOutput, calls=%fused_computation.6 | convolution fusion | flops 6444548096 | bytes 20971552 | tf_op jit(solution)/shard_map/sij,sjk->sik/dot_general | solution.py:149
  392.0 7.5 %fusion.6 = f32[2,256,256]{2,0,1:T(2,128)S(1)} fusion(f32[32,256,256]{2,1,0:T(8,128)S(1)} %fusion.2, pred[32]{0:T(512)(128)(4,1)S(1)} %broadcast_compare_fusion.2, s32[32]{0:T(128)S(1)} %get-tuple-element.45), kind=kOutput, calls=%fused_computation.10 | convolution fusion | flops 50331776 | bytes 8913056 | tf_op jit(solution)/shard_map/ps,sik->pik/dot_general | solution.py:152
  399.8 0.8 fusion.92
  403.4 0.9 convolution_add_fusion.8
  409.7 1.4 fusion.143
  411.1 55.6 %all-gather.5.cloned.1.call-done = bf16[64,256,256]{2,1,0:T(8,128)(2,1)} async-done(((bf16[2,256,256]{2,1,0:T(8,128)(2,1)}), bf16[64,256,256]{2,1,0:T(8,128)(2,1)}) %all-gather.5.cloned.1.call-update) | async-done | bytes 8388624 | tf_op jit(solution)/shard_map/all_gather | solution.py:147
  466.8 6.2 %gather_fusion.3 = bf16[32,256,256]{2,1,0:T(8,128)(2,1)} fusion(bf16[64,256,256]{2,1,0:T(8,128)(2,1)} %all-gather.5.cloned.1.call-done, s32[1024]{0:T(1024)S(1)} %pad_clamp_fusion), kind=kCustom, calls=%fused_computation.1.clone | custom fusion | bytes 8388736 | tf_op jit(solution)/shard_map/jit(_take)/gather | solution.py:148
  473.0 8.6 %fusion = f32[32,256,256]{2,1,0:T(8,128)S(1)} fusion(f32[32,1,256,256]{3,2,1,0:T(8,128)} %all-to-all-done.1, bf16[32,256,256]{2,1,0:T(8,128)(2,1)} %gather_fusion.3, pred[32]{0:T(512)(128)(4,1)S(1)} %compare_and_fusion.1), kind=kOutput, calls=%fused_computation.4 | convolution fusion | flops 6444548096 | bytes 20971552 | tf_op jit(solution)/shard_map/sij,sjk->sik/dot_general | solution.py:149
  481.6 7.5 %fusion.4 = f32[2,256,256]{2,0,1:T(2,128)S(1)} fusion(f32[32,256,256]{2,1,0:T(8,128)S(1)} %fusion, pred[32]{0:T(512)(128)(4,1)S(1)} %broadcast_compare_fusion.2, s32[32]{0:T(128)S(1)} %get-tuple-element.45), kind=kOutput, calls=%fused_computation.8 | convolution fusion | flops 50331776 | bytes 8913056 | tf_op jit(solution)/shard_map/ps,sik->pik/dot_general | solution.py:152
  489.4 0.8 fusion.89
  490.9 0.8 convolution_add_fusion.4
  493.0 1.1 convolution_add_fusion.3
  500.4 3.8 all_to_all.30
  504.5 16.8 %all_to_all.31 = f32[64,2,256]{2,1,0:T(2,128)S(1)} all-to-all(f32[64,2,256]{2,1,0:T(2,128)S(1)} %reduce_sum.127), channel_id=1, replica_groups=mesh['gx'=4,'gy_0'=4,'gy_1'=4,'gy_2'=2] {'gx','gy_0','gy_1'}, dimensions={0} | all-to-all | bytes 262144 | tf_op jit(solution)/shard_map/all_to_all | solution.py:57
  521.4 13.6 %all_to_all.32 = f32[64,2,256]{2,1,0:T(2,128)S(1)} all-to-all(f32[64,2,256]{2,1,0:T(2,128)S(1)} %broadcast_in_dim.34), channel_id=1, replica_groups=mesh['gx'=4,'gy_0'=4,'gy_1'=4,'gy_2'=2] {'gx','gy_0','gy_1'}, dimensions={0} | all-to-all | bytes 262144 | tf_op jit(solution)/shard_map/all_to_all | solution.py:24
  535.1 6.6 %all_to_all.33 = f32[2,64,2,256]{3,2,1,0:T(2,128)S(1)} all-to-all(f32[2,64,2,256]{3,2,1,0:T(2,128)S(1)} %broadcast_in_dim.35), channel_id=1, replica_groups=mesh['gx'=4,'gy_0'=4,'gy_1'=4,'gy_2'=2] {'gy_2'}, dimensions={0} | all-to-all | bytes 524288 | tf_op jit(solution)/shard_map/all_to_all | solution.py:24
  550.6 3.3 fusion.8
  553.9 6.3 %copy.217 = bf16[2,4096,256]{2,1,0:T(8,128)(2,1)} copy(bf16[2,4096,256]{1,2,0:T(8,128)(2,1)} %fusion.8) | data formatting | bytes 8388608
  (122 shorter events, 39.3 us)
Async XLA Ops:
  82.8 10.0 %copy-start.1 = (f32[2,256,256]{2,1,0:T(8,128)S(1)}, f32[2,256,256]{2,1,0:T(8,128)}, u32[]{:S(2)}) copy-start(f32[2,256,256]{2,1,0:T(8,128)} %param.9) | copy-start | bytes 1572868
  82.8 115.8 %all-to-all-start = ((bf16[32,1,512,256]{3,2,1,0:T(8,128)(2,1)}), bf16[32,1,512,256]{3,2,1,0:T(8,128)(2,1)}, u32[]{:S(2)}, u32[]{:S(2)}) async-start(bf16[32,1,512,256]{3,2,1,0:T(8,128)(2,1)} %broadcast_select_fusion), calls=%async_computation | async-start | bytes 16777216 | tf_op jit(solution)/shard_map/all_to_all | solution.py:117
  92.4 190.2 %all-gather.3.cloned.1.call-start = ((), (), s32[]{:S(2)}) async-start(), calls=%async_computation.6 | async-start | bytes 8650752 | tf_op jit(solution)/shard_map/all_gather | solution.py:147
  262.3 120.9 %all-to-all-start.1 = ((f32[32,1,256,256]{3,2,1,0:T(8,128)}), f32[32,1,256,256]{3,2,1,0:T(8,128)}, u32[]{:S(2)}, u32[]{:S(2)}) async-start(f32[32,1,256,256]{3,2,1,0:T(8,128)} %copy.204), calls=%async_computation.1 | async-start | bytes 16777216 | tf_op jit(solution)/shard_map/all_to_all | solution.py:141
  282.5 184.3 %all-gather.5.cloned.1.call-start = ((), (), s32[]{:S(2)}) async-start(), calls=%async_computation.7 | async-start | bytes 8650752 | tf_op jit(solution)/shard_map/all_gather | solution.py:147
  544.7 2.4 copy-start.3
  548.3 2.2 copy-start
  550.6 3.3 copy-start.2
Sparse Core Ops, SparseCore 0:
  104.2 109.6 all-gather.2
  411.3 55.4 all-gather.4
where the time goes:
time: 571 us; the launch traced here: 567 us
  waiting for transfers between devices  244 us (43%)
  matrix products  119 us (21%)
  local copies, waits for them, and re-layouts  104 us (18%)
  blocking collectives  40.8 us (7%)
  starting transfers between devices  30.1 us (5%)
  between operations  15.9 us (3%)
  other arithmetic  13.4 us (2%)
    all_to_all x1, waiting for transfers between devices, local(): lax.all_to_all(rotation_slots, GY, split_axis=0, concat_axis=0, tiled=True)  94.4 us
    all_to_all x1, waiting for transfers between devices, local(): lax.all_to_all(packed, GY, split_axis=0, concat_axis=0, tiled=True)  94.2 us
    gather x1, local copies, waits for them, and re-layouts, local(): jnp.take(patches.reshape(per_device * row_count, width), row_index, axis=0)  63.5 us
    all_gather x2, waiting for transfers between devices, local(): everyone = lax.all_gather(frames_low, GY, axis=0, tiled=True)  55.7 us
    dot_general x25, matrix products, newton_schulz(): jnp.einsum('...ij,...jk->...ik', polynom, matrix, precision=lax.Precision...  26.8 us
    dot_general x25, matrix products, newton_schulz(): jnp.einsum('...ij,...kj->...ik', matrix, matrix, precision=lax.Precision....  23.6 us
    dot_general x25, matrix products, newton_schulz(): jnp.einsum('...ij,...jk->...ik', square, square, precision=lax.Precision....  23.3 us
    all_to_all x2, blocking collectives, from_everyone(): lax.all_to_all(jnp.broadcast_to(value[None], (size, *value.shape)), axis,...  20.2 us
  transfers between devices with their start and end apart: 4, of which 3 were waited for; matrix products, arithmetic and copies ran while one was open for 14% of the time, Pallas kernels for 0%

commit v1 on v0

--- a/solution.py
+++ b/solution.py
@@ -144,7 +144,8 @@
     partner_flat = slot_partner.reshape(-1)
     for iteration in range(SWEEPS):
         frames_low = frames.astype(jnp.bfloat16)
-        everyone = lax.all_gather(frames_low, GY, axis=0, tiled=True)
+        stack = jnp.stack([frames_low] * lax.axis_size(GY))
+        everyone = jnp.concatenate(lax.all_to_all(stack, GY, 0, 0), axis=0)
         partner = jnp.take(everyone, partner_flat, axis=0).astype(jnp.float32)
         estimate = jnp.einsum(
             "sij,sjk->sik", rotation_recv, partner, precision=lax.Precision.HIGHEST

time: 571 us -> 643 us (1.13)
  blocking collectives: 40.8 us -> 146 us
  waiting for transfers between devices: 244 us -> 222 us
  between operations: 15.9 us -> 2.53 us
    all_to_all x0 -> x1, blocking collectives: none -> 105 us  [local(): everyone = jnp.concatenate(lax.all_to_all(stack, GY, 0, 0), axis=0)]
    all_gather x2 -> x0, waiting for transfers between devices: 55.7 us -> none  [local(): everyone = lax.all_gather(frames_low, GY, axis=0, tiled=True)]
    all_to_all x0 -> x1, waiting for transfers between devices: none -> 37.8 us  [local(): everyone = jnp.concatenate(lax.all_to_all(stack, GY, 0, 0), axis=0)]
    all_to_all x0 -> x1, starting transfers between devices: none -> 10.4 us  [local(): everyone = jnp.concatenate(lax.all_to_all(stack, GY, 0, 0), axis=0)]
    all_to_all x1, starting transfers between devices: 20.2 us -> 10.1 us  [local(): lax.all_to_all(rotation_slots, GY, split_axis=0, concat_axis=0, tiled=True)]
  transfers between devices with their start and end apart: 4 -> 3, of which waited for: 3 -> 3; matrix products, arithmetic and copies ran while one was open for 14% -> 12% of each run, Pallas kernels for 0% -> 0%
where the time goes in v1:
time: 643 us; the launch traced here: 640 us
  waiting for transfers between devices  222 us (35%)
  blocking collectives  146 us (23%)
  matrix products  117 us (18%)
  local copies, waits for them, and re-layouts  108 us (17%)
  starting transfers between devices  30.6 us (5%)
  other arithmetic  13.3 us (2%)
    all_to_all x1, blocking collectives, local(): everyone = jnp.concatenate(lax.all_to_all(stack, GY, 0, 0), axis=0)  105 us
    all_to_all x1, waiting for transfers between devices, local(): lax.all_to_all(rotation_slots, GY, split_axis=0, concat_axis=0, tiled=True)  94.4 us
    all_to_all x1, waiting for transfers between devices, local(): lax.all_to_all(packed, GY, split_axis=0, concat_axis=0, tiled=True)  90 us
    gather x1, local copies, waits for them, and re-layouts, local(): jnp.take(patches.reshape(per_device * row_count, width), row_index, axis=0)  63.5 us
    all_to_all x1, waiting for transfers between devices, local(): everyone = jnp.concatenate(lax.all_to_all(stack, GY, 0, 0), axis=0)  37.8 us
    dot_general x25, matrix products, newton_schulz(): jnp.einsum('...ij,...jk->...ik', polynom, matrix, precision=lax.Precision...  25.2 us
    dot_general x25, matrix products, newton_schulz(): jnp.einsum('...ij,...kj->...ik', matrix, matrix, precision=lax.Precision....  23.5 us
    dot_general x25, matrix products, newton_schulz(): jnp.einsum('...ij,...jk->...ik', square, square, precision=lax.Precision....  23 us
  transfers between devices with their start and end apart: 3, of which 3 were waited for; matrix products, arithmetic and copies ran while one was open for 12% of the time, Pallas kernels for 0%

profile of v1, /device:TPU:1, one launch (start us, length us, event | category | flops | bytes accessed | tf_op | source)
XLA Modules:
  0.0 639.6 jit_solution(5391340658357652676)
XLA Ops:
  3.2 0.9 copy.197
  4.7 63.5 %gather_fusion = bf16[16384,256]{1,0:T(8,128)(2,1)} fusion(bf16[8192,256]{1,0:T(8,128)(2,1)} %bitcast.208, s32[16384]{0:T(1024)S(1)} %broadcast_clamp_fusion), kind=kCustom, calls=%fused_computation.2 | custom fusion | bytes 16842752 | tf_op jit(solution)/shard_map/jit(_take)/gather | solution.py:115
  68.2 8.0 %broadcast_select_fusion = bf16[32,1,512,256]{3,2,1,0:T(8,128)(2,1)} fusion(bf16[32,1,512,256]{3,2,1,0:T(8,128)(2,1)} %bitcast.209, pred[32,512]{1,0:T(8,128)(4,1)S(1)} %compare_and_fusion), kind=kLoop, calls=%fused_computation.12 | loop fusion | flops 4194304 | bytes 16793600 | tf_op jit(solution)/shard_map/jit(_take)/select_n | solution.py:115
  76.2 10.1 %all-to-all-start = ((bf16[32,1,512,256]{3,2,1,0:T(8,128)(2,1)}), bf16[32,1,512,256]{3,2,1,0:T(8,128)(2,1)}, u32[]{:S(2)}, u32[]{:S(2)}) async-start(bf16[32,1,512,256]{3,2,1,0:T(8,128)(2,1)} %broadcast_select_fusion), calls=%async_computation | async-start | bytes 16777216 | tf_op jit(solution)/shard_map/all_to_all | solution.py:117
  96.9 90.0 %all-to-all-done = bf16[32,1,512,256]{3,2,1,0:T(8,128)(2,1)} async-done(((bf16[32,1,512,256]{3,2,1,0:T(8,128)(2,1)}), bf16[32,1,512,256]{3,2,1,0:T(8,128)(2,1)}, u32[]{:S(2)}, u32[]{:S(2)}) %all-to-all-start) | async-done | bytes 8388640 | tf_op jit(solution)/shard_map/all_to_all | solution.py:117
  187.0 4.2 stack.13
  191.2 10.4 %all-to-all-start.2 = ((bf16[32,2,256,256]{3,2,1,0:T(8,128)(2,1)}), bf16[32,2,256,256]{3,2,1,0:T(8,128)(2,1)}, u32[]{:S(2)}, u32[]{:S(2)}) async-start(bf16[32,2,256,256]{3,2,1,0:T(8,128)(2,1)} %stack.13), calls=%async_computation.2 | async-start | bytes 16777216 | tf_op jit(solution)/shard_map/all_to_all | solution.py:148
  202.0 6.2 gather_fusion.1
  208.2 3.1 multiply_reduce_fusion
  211.3 2.3 fusion.48
  213.6 2.1 fusion.149
  215.8 2.6 multiply_add_fusion.4
  218.4 2.1 fusion.150
  220.5 2.3 fusion.151
  222.9 2.4 multiply_add_fusion.3
  225.3 2.1 fusion.152
  227.4 2.1 fusion.153
  229.6 2.4 multiply_add_fusion.2
  232.0 2.5 fusion.154
  234.5 2.1 fusion.155
  236.7 2.4 multiply_add_fusion.1
  239.1 2.1 fusion.156
  241.2 2.1 fusion.157
  243.3 2.4 multiply_add_fusion
  245.8 2.0 copy.201
  247.7 2.0 pad_maximum_fusion
  250.1 5.7 fusion.15
  255.9 8.1 %copy.204 = f32[32,1,256,256]{3,2,1,0:T(8,128)} copy(f32[32,1,256,256]{3,0,2,1:T(8,128)S(1)} %fusion.15) | data formatting | bytes 16777216 | tf_op jit(solution)/shard_map/dce,eij->dcij/dot_general | solution.py:140
  263.9 37.8 %all-to-all-done.2 = bf16[32,2,256,256]{3,2,1,0:T(8,128)(2,1)} async-done(((bf16[32,2,256,256]{3,2,1,0:T(8,128)(2,1)}), bf16[32,2,256,256]{3,2,1,0:T(8,128)(2,1)}, u32[]{:S(2)}, u32[]{:S(2)}) %all-to-all-start.2) | async-done | bytes 8388640 | tf_op jit(solution)/shard_map/all_to_all | solution.py:148
  301.8 10.1 %all-to-all-start.1 = ((f32[32,1,256,256]{3,2,1,0:T(8,128)}), f32[32,1,256,256]{3,2,1,0:T(8,128)}, u32[]{:S(2)}, u32[]{:S(2)}) async-start(f32[32,1,256,256]{3,2,1,0:T(8,128)} %copy.204), calls=%async_computation.1 | async-start | bytes 16777216 | tf_op jit(solution)/shard_map/all_to_all | solution.py:141
  312.0 6.2 gather_fusion.2
  318.2 94.4 %all-to-all-done.1 = f32[32,1,256,256]{3,2,1,0:T(8,128)} async-done(((f32[32,1,256,256]{3,2,1,0:T(8,128)}), f32[32,1,256,256]{3,2,1,0:T(8,128)}, u32[]{:S(2)}, u32[]{:S(2)}) %all-to-all-start.1) | async-done | bytes 8388640 | tf_op jit(solution)/shard_map/all_to_all | solution.py:141
  412.6 8.8 %fusion.2 = f32[32,256,256]{2,1,0:T(8,128)S(1)} fusion(f32[32,1,256,256]{3,2,1,0:T(8,128)} %all-to-all-done.1, bf16[32,256,256]{2,1,0:T(8,128)(2,1)} %gather_fusion.2, pred[32]{0:T(512)(128)(4,1)S(1)} %compare_and_fusion.1), kind=kOutput, calls=%fused_computation.6 | convolution fusion | flops 6444548096 | bytes 20971552 | tf_op jit(solution)/shard_map/sij,sjk->sik/dot_general | solution.py:150
  421.5 7.5 %fusion.6 = f32[2,256,256]{2,0,1:T(2,128)S(1)} fusion(f32[32,256,256]{2,1,0:T(8,128)S(1)} %fusion.2, pred[32]{0:T(512)(128)(4,1)S(1)} %broadcast_compare_fusion.2, s32[32]{0:T(128)S(1)} %get-tuple-element.45), kind=kOutput, calls=%fused_computation.10 | convolution fusion | flops 50331776 | bytes 8913056 | tf_op jit(solution)/shard_map/ps,sik->pik/dot_general | solution.py:153
  429.2 0.8 fusion.92
  432.8 0.9 convolution_add_fusion.8
  439.8 1.0 stack.14
  440.8 104.8 %all_to_all.40 = bf16[32,2,256,256]{3,2,1,0:T(8,128)(2,1)} all-to-all(bf16[32,2,256,256]{3,2,1,0:T(8,128)(2,1)S(1)} %stack.14), channel_id=1, replica_groups=mesh['gx'=4,'gy_0'=4,'gy_1'=4,'gy_2'=2] {'gy_0','gy_1','gy_2'}, dimensions={0} | all-to-all | bytes 16777216 | tf_op jit(solution)/shard_map/all_to_all | solution.py:148
  545.7 6.2 gather_fusion.3
  551.9 8.6 %fusion = f32[32,256,256]{2,1,0:T(8,128)S(1)} fusion(f32[32,1,256,256]{3,2,1,0:T(8,128)} %all-to-all-done.1, bf16[32,256,256]{2,1,0:T(8,128)(2,1)} %gather_fusion.3, pred[32]{0:T(512)(128)(4,1)S(1)} %compare_and_fusion.1), kind=kOutput, calls=%fused_computation.4 | convolution fusion | flops 6444548096 | bytes 20971552 | tf_op jit(solution)/shard_map/sij,sjk->sik/dot_general | solution.py:150
  560.5 7.5 %fusion.4 = f32[2,256,256]{2,0,1:T(2,128)S(1)} fusion(f32[32,256,256]{2,1,0:T(8,128)S(1)} %fusion, pred[32]{0:T(512)(128)(4,1)S(1)} %broadcast_compare_fusion.2, s32[32]{0:T(128)S(1)} %get-tuple-element.45), kind=kOutput, calls=%fused_computation.8 | convolution fusion | flops 50331776 | bytes 8913056 | tf_op jit(solution)/shard_map/ps,sik->pik/dot_general | solution.py:153
  571.9 1.1 convolution_add_fusion.3
  579.3 4.0 all_to_all.41
  583.5 17.0 %all_to_all.42 = f32[64,2,256]{2,1,0:T(2,128)S(1)} all-to-all(f32[64,2,256]{2,1,0:T(2,128)S(1)} %reduce_sum.127), channel_id=1, replica_groups=mesh['gx'=4,'gy_0'=4,'gy_1'=4,'gy_2'=2] {'gx','gy_0','gy_1'}, dimensions={0} | all-to-all | bytes 262144 | tf_op jit(solution)/shard_map/all_to_all | solution.py:57
  600.6 13.6 %all_to_all.43 = f32[64,2,256]{2,1,0:T(2,128)S(1)} all-to-all(f32[64,2,256]{2,1,0:T(2,128)S(1)} %broadcast_in_dim.34), channel_id=1, replica_groups=mesh['gx'=4,'gy_0'=4,'gy_1'=4,'gy_2'=2] {'gx','gy_0','gy_1'}, dimensions={0} | all-to-all | bytes 262144 | tf_op jit(solution)/shard_map/all_to_all | solution.py:24
  614.3 6.6 %all_to_all.44 = f32[2,64,2,256]{3,2,1,0:T(2,128)S(1)} all-to-all(f32[2,64,2,256]{3,2,1,0:T(2,128)S(1)} %broadcast_in_dim.35), channel_id=1, replica_groups=mesh['gx'=4,'gy_0'=4,'gy_1'=4,'gy_2'=2] {'gy_2'}, dimensions={0} | all-to-all | bytes 524288 | tf_op jit(solution)/shard_map/all_to_all | solution.py:24
  629.8 3.3 fusion.8
  633.1 6.3 copy.217
  (121 shorter events, 41.8 us)
Async XLA Ops:
  76.2 10.1 %copy-start.1 = (f32[2,256,256]{2,1,0:T(8,128)S(1)}, f32[2,256,256]{2,1,0:T(8,128)}, u32[]{:S(2)}) copy-start(f32[2,256,256]{2,1,0:T(8,128)} %param.9) | copy-start | bytes 1572868
  76.2 110.7 %all-to-all-start = ((bf16[32,1,512,256]{3,2,1,0:T(8,128)(2,1)}), bf16[32,1,512,256]{3,2,1,0:T(8,128)(2,1)}, u32[]{:S(2)}, u32[]{:S(2)}) async-start(bf16[32,1,512,256]{3,2,1,0:T(8,128)(2,1)} %broadcast_select_fusion), calls=%async_computation | async-start | bytes 16777216 | tf_op jit(solution)/shard_map/all_to_all | solution.py:117
  191.2 110.6 %all-to-all-start.2 = ((bf16[32,2,256,256]{3,2,1,0:T(8,128)(2,1)}), bf16[32,2,256,256]{3,2,1,0:T(8,128)(2,1)}, u32[]{:S(2)}, u32[]{:S(2)}) async-start(bf16[32,2,256,256]{3,2,1,0:T(8,128)(2,1)} %stack.13), calls=%async_computation.2 | async-start | bytes 16777216 | tf_op jit(solution)/shard_map/all_to_all | solution.py:148
  301.8 110.9 %all-to-all-start.1 = ((f32[32,1,256,256]{3,2,1,0:T(8,128)}), f32[32,1,256,256]{3,2,1,0:T(8,128)}, u32[]{:S(2)}, u32[]{:S(2)}) async-start(f32[32,1,256,256]{3,2,1,0:T(8,128)} %copy.204), calls=%async_computation.1 | async-start | bytes 16777216 | tf_op jit(solution)/shard_map/all_to_all | solution.py:141
  622.7 2.1 copy-start.3
  627.5 2.2 copy-start
  629.7 3.3 copy-start.2
